TPU v7x, 256 devices: a whole 4x4x8 slice. The times are simulated.
256 devices in a mesh: query: 16 (over z, y_lo), db: 16 (over x, y_hi, core).
Axes of the slice: x: 4, y: 4 (y_hi: 2, y_lo: 2; y = y_hi * 2 + y_lo), z: 8, core: 2. Of those that a mesh axis runs over, the one named last changes fastest.
Arguments:
- noisy_images: float32 [16, 3, 128, 128], P('db', None, 'query'), may hold values from -6 to 6
- database: bfloat16 [432, 262144], P(None, 'db'), may hold values from -4 to 4
- picked_blocks: int32 [16, 4], P('db'), may hold values from 0 to 7, as said below
- alpha_now: float32 [16], replicated, may hold values from 0.15 to 0.35
- alpha_next: float32 [16], replicated, may hold values from 0.4 to 0.8
Outputs:
- next_images: float32 [16, 3, 128, 128], P('db', None, 'query')
Inputs may be any that keep to these rules, and one draw needn't show every extreme that they name: `picked_blocks`: each row names 4 different windows of the 8 stored on that shard.
All inputs are finite; a program needn't handle non-finite values.
Results may differ from a plain program's by a relative error of at most 0.00075.
Values may be sent and summed in bfloat16 or wider, within the bound.
A program may use at most 192 MiB of HBM per device.

v0:
```python
import jax
import jax.numpy as jnp
from jax import lax
from jax.sharding import PartitionSpec as P

BLOCK = 2048


def shifted(value, axis, by):
    count = lax.axis_size(axis)
    return lax.ppermute(value, axis, [(i, (i + by) % count) for i in range(count)])


def combined_all(value, axis, combine):
    everything = jax.tree.map(lambda part: lax.all_gather(part, axis), value)
    first = jax.tree.map(lambda part: part[0], everything)

    def lap(k, so_far):
        return combine(so_far, jax.tree.map(lambda part: part[k], everything))

    return lax.fori_loop(1, lax.axis_size(axis), lap, first)


def extract(pixels):
    height = pixels.shape[2] - 8
    across = pixels.shape[3] - 8
    slab_list = []
    for row_shift in range(12):
        for col_shift in range(12):
            slab_list.append(
                pixels[:, :, row_shift : row_shift + height : 4, col_shift : col_shift + across : 4]
            )
    stacked = jnp.stack(slab_list)
    stacked = stacked.reshape(12, 12, stacked.shape[1], 3, stacked.shape[3], stacked.shape[4])
    stacked = jnp.transpose(stacked, (3, 0, 1, 2, 4, 5))
    return stacked.reshape(432, -1)


def combine(first, second):
    top = jnp.maximum(first[0], second[0])
    factor_one = jnp.exp(first[0] - top)
    factor_two = jnp.exp(second[0] - top)
    totals = first[1] * factor_one + second[1] * factor_two
    numerator = first[2] * factor_one[None, :] + second[2] * factor_two[None, :]
    return (top, totals, numerator)


def on_device(noisy_images, database, picked_blocks, alpha_now, alpha_next):
    images_dev, channels, height, across = noisy_images.shape
    rounded = noisy_images.astype(jnp.bfloat16)
    below = shifted(rounded, "query", -1)
    extended = jnp.concatenate([rounded, below], axis=2)
    extended = jnp.concatenate([extended, extended[:, :, :, :8]], axis=3)
    per_image = height // 4 * (across // 4)
    gathered = lax.all_gather(extract(extended), "db", axis=1, tiled=True)
    count = gathered.shape[1]
    per_query = jnp.repeat(alpha_now, per_image)
    linear = jnp.sqrt(per_query) / (1.0 - per_query)
    quadratic = per_query / (2.0 * (1.0 - per_query))
    maxima = jnp.full((count,), -jnp.inf, jnp.float32)
    totals = jnp.zeros((count,), jnp.float32)
    numerator = jnp.zeros((432, count), jnp.float32)
    for slot in range(picked_blocks.shape[1]):
        offset = picked_blocks[0, slot] * BLOCK
        window = lax.dynamic_slice_in_dim(database, offset, BLOCK, 1)
        squares = jnp.sum(window.astype(jnp.float32) ** 2, axis=0)
        inner = lax.dot_general(
            gathered, window, (((0,), (0,)), ((), ())), preferred_element_type=jnp.float32
        )
        logits = linear[:, None] * inner - quadratic[:, None] * squares[None, :]
        new_max = jnp.maximum(maxima, jnp.max(logits, axis=1))
        rescale = jnp.exp(maxima - new_max)
        raw = jnp.exp(logits - new_max[:, None])
        totals = totals * rescale + jnp.sum(raw, axis=1)
        weighted = lax.dot_general(
            window,
            raw.astype(jnp.bfloat16),
            (((1,), (1,)), ((), ())),
            preferred_element_type=jnp.float32,
        )
        numerator = numerator * rescale[None, :] + weighted
        maxima = new_max
    per_device = images_dev * per_image
    maxima, totals, numerator = combined_all((maxima, totals, numerator), "db", combine)
    own_start = lax.axis_index("db") * per_device
    totals = lax.dynamic_slice_in_dim(totals, own_start, per_device, 0)
    numerator = lax.dynamic_slice_in_dim(numerator, own_start, per_device, 1)
    estimate = numerator / totals[None, :]
    pieces = estimate.reshape(3, 3, 4, 3, 4, images_dev, height // 4, across // 4)
    accum = jnp.zeros((images_dev, 3, height // 4 + 2, 4, across // 4 + 2, 4), jnp.float32)
    for coarse_row in range(3):
        for coarse_col in range(3):
            piece = jnp.transpose(pieces[:, coarse_row, :, coarse_col], (3, 0, 4, 1, 5, 2))
            accum = accum + jnp.pad(
                piece,
                (
                    (0, 0),
                    (0, 0),
                    (coarse_row, 2 - coarse_row),
                    (0, 0),
                    (coarse_col, 2 - coarse_col),
                    (0, 0),
                ),
            )
    summed = accum.reshape(images_dev, 3, height + 8, across + 8)
    summed = summed[:, :, :, :across].at[:, :, :, :8].add(summed[:, :, :, across:])
    spill = shifted(summed[:, :, height:, :], "query", 1)
    denoised = summed[:, :, :height, :].at[:, :, :8, :].add(spill) / 9.0
    own_images = lax.axis_index("db") * images_dev
    signal = lax.dynamic_slice_in_dim(alpha_now, own_images, images_dev, 0)[:, None, None, None]
    after = lax.dynamic_slice_in_dim(alpha_next, own_images, images_dev, 0)[:, None, None, None]
    noise_part = (noisy_images - jnp.sqrt(signal) * denoised) / jnp.sqrt(1.0 - signal)
    return jnp.sqrt(after) * denoised + jnp.sqrt(1.0 - after) * noise_part


def solution(mesh):
    return jax.shard_map(
        on_device,
        mesh=mesh,
        in_specs=(P("db", None, "query", None), P(None, "db"), P("db", None), P(), P()),
        out_specs=P("db", None, "query", None),
        check_vma=False,
    )
```

profile of v0, /device:TPU:1, one launch (start us, length us, event | category | flops | bytes accessed | tf_op | source)
XLA Modules:
  0.0 337.6 jit_solution(15268145274604213155)
XLA Ops:
  6.5 0.7 convert_element_type.45
  7.2 7.4 %collective-permute-start = (bf16[1,3,8,128]{3,2,1,0:T(8,128)(2,1)S(1)}, bf16[1,3,8,128]{3,2,1,0:T(8,128)(2,1)S(1)}, u32[]{:S(2)}, u32[]{:S(2)}) collective-permute-start(bf16[1,3,8,128]{3,2,1,0:T(8,128)(2,1)S(1)} %convert_element_type.45), channel_id=1, source_target_pairs={{0,240},{16,0},{32,16},{48,32},{64,48},{80,64},{96,80},{112,96},{1... | collective-permute-start | bytes 18440 | tf_op jit(solution)/shard_map/ppermute | solution.py:11
  14.7 1.5 fusion.44
  18.9 0.7 broadcast_in_dim.14
  19.7 4.7 %multiply_reduce_fusion.2 = (f32[2048]{0:T(1024)S(1)}, f32[2048]{0:T(1024)S(1)}, f32[2048]{0:T(1024)S(1)}, f32[2048]{0:T(1024)S(1)}) fusion(bf16[432,16384]{1,0:T(8,128)(2,1)} %param.14, s32[]{:T(128)S(6)} %select_n.33, s32[]{:T(128)S(6)} %select_n.32, s32[]{:T(128)S(6)} %select_n.34, s32[]{:T(128)S(6)} %select_n.35), kind=kLoop, calls=%fused_computation.33 | loop fusion | flops 10608640 | bytes 7110672 | tf_op jit(solution)/shard_map/reduce_sum | solution.py:66
  24.4 0.1 slice.610
  24.5 0.1 slice.598
  24.6 0.1 slice.586
  24.8 0.1 slice.574
  24.9 0.1 slice.562
  25.0 0.1 slice.634
  25.2 0.1 slice.622
  31.1 0.1 slice.643
  31.3 0.1 slice.642
  31.6 0.1 slice.639
  32.2 0.1 slice.635
  32.5 0.1 slice.631
  32.7 0.1 slice.630
  33.1 0.1 slice.627
  33.2 0.1 slice.626
  33.6 0.1 slice.623
  44.0 0.3 slice.670
  44.7 0.2 copy.4667
  44.8 0.1 reshape.299
  45.1 27.8 %all_gather.17 = bf16[432,1024]{0,1:T(8,128)(2,1)S(1)} all-gather(bf16[432,64]{0,1:T(8,128)(2,1)S(1)} %copy.4668), channel_id=1, replica_groups=mesh['query'=16,'db'=16] {'db'}, dimensions={1}, use_global_device_ids=true | all-gather | bytes 940032 | tf_op jit(solution)/shard_map/all_gather | solution.py:55
  72.9 3.8 %fusion.24 = f32[1024,2048]{1,0:T(8,128)S(1)} fusion(bf16[432,1024]{0,1:T(8,128)(2,1)S(1)} %all_gather.17, bf16[432,16384]{1,0:T(8,128)(2,1)} %param.14, s32[]{:T(128)S(6)} %select_n.35), kind=kOutput, calls=%fused_computation.37 | convolution fusion | flops 1811939328 | bytes 11042820 | tf_op jit(solution)/shard_map/dot_general | solution.py:67
  76.8 8.5 %fusion.27 = f32[1024,2048]{1,0:T(8,128)} fusion(bf16[432,1024]{0,1:T(8,128)(2,1)S(1)} %all_gather.17, bf16[432,16384]{1,0:T(8,128)(2,1)} %param.14, s32[]{:T(128)S(6)} %select_n.34), kind=kOutput, calls=%fused_computation.40 | convolution fusion | flops 1811939328 | bytes 11042820 | tf_op jit(solution)/shard_map/dot_general | solution.py:67
  85.2 6.5 %fusion.9 = (f32[1024]{0:T(1024)S(1)}, f32[1024,2048]{1,0:T(8,128)}) fusion(f32[2048]{0:T(1024)S(1)} %get-tuple-element.217, f32[1024]{0:T(1024)S(1)} %get-tuple-element.266, f32[1024]{0:T(1024)S(1)} %get-tuple-element.265, bf16[432,1024]{0,1:T(8,128)(2,1)S(1)} %all_gather.17, bf16[432,16384]{1,0:T(8,128)(2,1)} %param.14, s32[]{:T(128)S(6)} %select_n.32), kind=kOutput, calls=%fused_computation.23 | convolution fusion | flops 1820326912 | bytes 11063300 | tf_op jit(solution)/shard_map/dot_general | solution.py:67
  91.7 12.9 %fusion.2 = (f32[1024]{0:T(1024)S(1)}, f32[1024]{0:T(1024)S(1)}, f32[1024]{0:T(1024)S(1)}, f32[1024]{0:T(1024)S(1)}, f32[1024,2048]{1,0:T(8,128)}) fusion(f32[1024,2048]{1,0:T(8,128)} %get-tuple-element.272, f32[1024]{0:T(1024)S(1)} %get-tuple-element.271, f32[2048]{0:T(1024)S(1)} %get-tuple-element.217, f32[1024]{0:T(1024)S(1)} %get-tuple-element.266, ...), kind=kOutput, calls=%fused_computation.16 | convolution fusion | flops 1847586816 | bytes 36270084 | tf_op jit(solution)/shard_map/dot_general | solution.py:67
  104.7 5.8 %fusion.15 = f32[432,1024]{1,0:T(8,128)S(1)} fusion(f32[1024,2048]{1,0:T(8,128)} %fusion.27, f32[1024]{0:T(1024)S(1)} %get-tuple-element.248, f32[2048]{0:T(1024)S(1)} %get-tuple-element.218, f32[1024]{0:T(1024)S(1)} %get-tuple-element.266, f32[1024]{0:T(1024)S(1)} %get-tuple-element.265, bf16[432,16384]{1,0:T(8,128)(2,1)} %param.14, s32[]{:T(128)S(6)} %select_n.34), kind=kOutput, calls=%fused_computation.28 | convolution fusion | flops 1822425088 | bytes 11948036 | tf_op jit(solution)/shard_map/dot_general | solution.py:75
  110.6 4.3 %fusion.13 = f32[432,1024]{1,0:T(8,128)S(1)} fusion(f32[1024,2048]{1,0:T(8,128)S(1)} %fusion.24, f32[1024]{0:T(1024)S(1)} %get-tuple-element.250, f32[2048]{0:T(1024)S(1)} %get-tuple-element.219, f32[1024]{0:T(1024)S(1)} %get-tuple-element.266, f32[1024]{0:T(1024)S(1)} %get-tuple-element.265, bf16[432,16384]{1,0:T(8,128)(2,1)} %param.14, s32[]{:T(128)S(6)} %select_n.35), kind=kOutput, calls=%fused_computation.27 | convolution fusion | flops 1822425088 | bytes 11948036 | tf_op jit(solution)/shard_map/dot_general | solution.py:75
  115.0 4.3 %fusion.17 = f32[432,1024]{1,0:T(8,128)S(1)} fusion(f32[1024,2048]{1,0:T(8,128)S(1)} %bitcast.375, f32[1024]{0:T(1024)S(1)} %get-tuple-element.246, f32[2048]{0:T(1024)S(1)} %get-tuple-element.216, f32[1024]{0:T(1024)S(1)} %get-tuple-element.266, f32[1024]{0:T(1024)S(1)} %get-tuple-element.265, bf16[432,16384]{1,0:T(8,128)(2,1)} %param.14, s32[]{:T(128)S(6)} %select_n.33), kind=kOutput, calls=%fused_computation.29 | convolution fusion | flops 1822425088 | bytes 11948036 | tf_op jit(solution)/shard_map/dot_general | solution.py:75
  119.3 6.3 %multiply_add_fusion.1 = f32[432,1024]{1,0:T(8,128)} fusion(f32[432,1024]{1,0:T(8,128)S(1)} %fusion.13, f32[432,1024]{1,0:T(8,128)S(1)} %fusion.15, f32[432,1024]{1,0:T(8,128)S(1)} %fusion.17, f32[1024,2048]{1,0:T(8,128)S(1)} %bitcast.393, f32[1024]{0:T(1024)S(1)} %get-tuple-element.271, f32[2048]{0:T(1024)S(1)} %get-tuple-element.217, ...), kind=kOutput, calls=%fused_computation.35 | convolution fusion | flops 1825521664 | bytes 17272836 | tf_op jit(solution)/shard_map/dot_general | solution.py:75
  125.7 12.2 %fusion.4 = (f32[1024]{0:T(1024)S(1)}, f32[1024]{0:T(1024)S(1)}, f32[1024]{0:T(1024)S(1)}) fusion(f32[1024,2048]{1,0:T(8,128)} %get-tuple-element.273, f32[1024]{0:T(1024)S(1)} %get-tuple-element.246, f32[2048]{0:T(1024)S(1)} %get-tuple-element.216, f32[1024]{0:T(1024)S(1)} %get-tuple-element.266, f32[1024]{0:T(1024)S(1)} %get-tuple-element.265, ...), kind=kLoop, calls=%fused_computation.18 | loop fusion | flops 31454208 | bytes 25223168 | tf_op jit(solution)/shard_map/reduce_sum | solution.py:74
  137.9 20.0 %all-gather.2 = f32[16,1,1024]{2,1,0:T(1,128)S(1)} all-gather(f32[1,1,1024]{2,1,0:T(1,128)S(1)} %get-tuple-element.262), channel_id=1, replica_groups=mesh['query'=16,'db'=16] {'db'}, dimensions={0}, use_global_device_ids=true | all-gather | bytes 69632 | tf_op jit(solution)/shard_map/all_gather | solution.py:15
  157.9 22.7 %all-gather.1 = f32[16,1,1024]{2,1,0:T(1,128)S(1)} all-gather(f32[1,1,1024]{2,1,0:T(1,128)S(1)} %get-tuple-element.263), channel_id=1, replica_groups=mesh['query'=16,'db'=16] {'db'}, dimensions={0}, use_global_device_ids=true | all-gather | bytes 69632 | tf_op jit(solution)/shard_map/all_gather | solution.py:15
  180.6 106.3 %all-gather.5.cloned.1.call-done = f32[6912,1024]{1,0:T(8,128)} async-done(((f32[432,1024]{1,0:T(8,128)}), f32[6912,1024]{1,0:T(8,128)}) %all-gather.5.cloned.1.call-update) | async-done | bytes 28311568 | tf_op jit(solution)/shard_map/all_gather | solution.py:15
  286.9 1.6 slice.722
  288.5 34.9 %while.22 = (s32[]{:T(128)}, f32[1024]{0:T(1024)S(1)}, f32[1024]{0:T(1024)S(1)}, f32[432,1024]{1,0:T(8,128)S(1)}, f32[16,1024]{1,0:T(8,128)S(1)}, /*index=5*/f32...) while((s32[]{:T(128)}, f32[1024]{0:T(1024)S(1)}, f32[1024]{0:T(1024)S(1)}, ...), condition=%wide.region_13.0_spmd, body=%wide.region_12.0_spmd.sunk | while | flops 1333253 | bytes 5365903 | solution.py:21
  288.6 2.3 fusion.50
  290.9 2.3 fusion.50
  293.2 2.3 fusion.50
  295.6 2.3 fusion.50
  297.9 2.3 fusion.50
  300.2 2.3 fusion.50
  302.5 2.3 fusion.50
  304.9 2.3 fusion.50
  307.2 2.3 fusion.50
  309.5 2.3 fusion.50
  311.9 2.3 fusion.50
  314.2 2.3 fusion.50
  316.5 2.3 fusion.50
  318.8 2.3 fusion.50
  321.2 2.3 fusion.50
  323.7 0.3 reshape.300
  324.0 0.4 pad_add_fusion
  324.4 0.5 copy.4669
  324.8 0.3 reshape.301
  325.1 0.3 scatter-add.4
  325.4 0.4 collective-permute-start.1
  325.8 0.6 dynamic_slice.61
  327.7 0.6 dynamic_slice.60
  329.8 0.4 collective-permute-done.1
  330.2 0.6 multiply_add_fusion.2
  (342 shorter events, 18.7 us)
Async XLA Ops:
  6.5 280.3 %all-gather.5.cloned.1.call-start = ((), (), s32[]{:S(2)}) async-start(), calls=%async_computation | async-start | bytes 30081024 | tf_op jit(solution)/shard_map/all_gather | solution.py:15
  7.2 17.1 %collective-permute-start = (bf16[1,3,8,128]{3,2,1,0:T(8,128)(2,1)S(1)}, bf16[1,3,8,128]{3,2,1,0:T(8,128)(2,1)S(1)}, u32[]{:S(2)}, u32[]{:S(2)}) collective-permute-start(bf16[1,3,8,128]{3,2,1,0:T(8,128)(2,1)S(1)} %convert_element_type.45), channel_id=1, source_target_pairs={{0,240},{16,0},{32,16},{48,32},{64,48},{80,64},{96,80},{112,96},{1... | collective-permute-start | bytes 18440 | tf_op jit(solution)/shard_map/ppermute | solution.py:11
  76.7 33.8 %copy-start = (f32[1024,2048]{1,0:T(8,128)}, f32[1024,2048]{1,0:T(8,128)S(1)}, u32[]{:S(2)}) copy-start(f32[1024,2048]{1,0:T(8,128)S(1)} %fusion.24) | copy-start | bytes 25165828
  104.7 10.2 %slice-start = ((s8[8388608]{0:T(1024)(128)(4,1)}), s8[4194304]{0:T(1024)(128)(4,1)S(1)}, s32[]{:S(2)}) async-start(s8[8388608]{0:T(1024)(128)(4,1)} %bitcast.374), calls=%async_computation.1 | async-start | bytes 8388608
  110.6 4.4 %slice-start.1 = ((s8[8388608]{0:T(1024)(128)(4,1)}), s8[4194304]{0:T(1024)(128)(4,1)S(1)}, s32[]{:S(2)}) async-start(s8[8388608]{0:T(1024)(128)(4,1)} %bitcast.374), calls=%async_computation.2 | async-start | bytes 8388608
  110.6 8.7 %slice-start.2 = ((s8[8388608]{0:T(1024)(128)(4,1)}), s8[4194304]{0:T(1024)(128)(4,1)S(1)}, s32[]{:S(2)}) async-start(s8[8388608]{0:T(1024)(128)(4,1)} %bitcast.392), calls=%async_computation.3 | async-start | bytes 8388608
  115.0 4.3 %slice-start.3 = ((s8[8388608]{0:T(1024)(128)(4,1)}), s8[4194304]{0:T(1024)(128)(4,1)S(1)}, s32[]{:S(2)}) async-start(s8[8388608]{0:T(1024)(128)(4,1)} %bitcast.392), calls=%async_computation.4 | async-start | bytes 8388608
  288.5 37.3 %copy-start.2 = (f32[16]{0:T(128)S(1)}, f32[16]{0:T(128)}, u32[]{:S(2)}) copy-start(f32[16]{0:T(128)} %param.16) | copy-start | bytes 196
  288.5 39.2 %copy-start.3 = (f32[16]{0:T(128)S(1)}, f32[16]{0:T(128)}, u32[]{:S(2)}) copy-start(f32[16]{0:T(128)} %param.17) | copy-start | bytes 196
  288.5 41.7 %copy-start.1 = (f32[1,3,8,128]{3,2,1,0:T(8,128)S(1)}, f32[1,3,8,128]{3,2,1,0:T(8,128)}, u32[]{:S(2)}) copy-start(f32[1,3,8,128]{3,2,1,0:T(8,128)} %param.13) | copy-start | bytes 36868
  325.4 4.7 %collective-permute-start.1 = (f32[1,3,8,128]{3,2,1,0:T(8,128)S(1)}, f32[1,3,8,128]{3,2,1,0:T(8,128)S(1)}, u32[]{:S(2)}, u32[]{:S(2)}) collective-permute-start(f32[1,3,8,128]{3,2,1,0:T(8,128)S(1)} %slice.736), channel_id=1, source_target_pairs={{0,16},{16,32},{32,48},{48,64},{64,80},{80,96},{96,112},{112,128},... | collective-permute-start | bytes 36872 | tf_op jit(solution)/shard_map/ppermute | solution.py:11
Sparse Core Ops, SparseCore 0:
  125.8 161.0 all-gather.4
where the time goes:
time: 338 us
  waiting for transfers between devices  107 us (32%)
  blocking collectives  70.5 us (21%)
  other arithmetic  53 us (16%)
  matrix products  52.5 us (16%)
  local copies, waits for them, and re-layouts  27.1 us (8%)
  between operations  19.5 us (6%)
  starting transfers between devices  7.79 us (2%)
    all_gather x1, waiting for transfers between devices, combined_all(): everything = jax.tree.map(lambda part: lax.all_gather(part, axis), value)  106 us
    all_gather x2, blocking collectives, combined_all(): everything = jax.tree.map(lambda part: lax.all_gather(part, axis), value)  42.7 us
    add x15, other arithmetic, combine(): numerator = first[2] * factor_one[None, :] + second[2] * factor_two[None, :]  34 us
    dot_general x4, matrix products, on_device(): lax.dot_general(gathered, window, (((0,), (0,)), ((), ())), preferred_ele...  31.7 us
    all_gather x1, blocking collectives, on_device(): gathered = lax.all_gather(extract(extended), 'db', axis=1, tiled=True)  27.8 us
    dot_general x4, matrix products, on_device(): lax.dot_general(window, raw.astype(jnp.bfloat16), (((1,), (1,)), ((), ())...  20.8 us
    slice x144, local copies, waits for them, and re-layouts, extract(): pixels[:, :, row_shift:row_shift + height:4, col_shift:col_shift + across:4]  18.4 us
    reduce_sum x1, other arithmetic, on_device(): totals = totals * rescale + jnp.sum(raw, axis=1)  12.2 us
  transfers between devices with their start and end apart: 3, of which 2 were waited for; matrix products, arithmetic and copies ran while one was open for 6% of the time, Pallas kernels for 0%

commit v1 on v0

--- a/solution.py
+++ b/solution.py
@@ -52,7 +52,16 @@
     extended = jnp.concatenate([rounded, below], axis=2)
     extended = jnp.concatenate([extended, extended[:, :, :, :8]], axis=3)
     per_image = height // 4 * (across // 4)
-    gathered = lax.all_gather(extract(extended), "db", axis=1, tiled=True)
+    launch_thing = lambda original, ndim_at: jnp.concatenate(
+        jax.lax.all_to_all(
+            jnp.stack(jax.lax.axis_size("db") * [original], axis=0),
+            axis_name="db",
+            split_axis=0,
+            concat_axis=0,
+        ),
+        axis=ndim_at,
+    )
+    gathered = launch_thing(extract(extended), 1)
     count = gathered.shape[1]
     per_query = jnp.repeat(alpha_now, per_image)
     linear = jnp.sqrt(per_query) / (1.0 - per_query)

time: 338 us -> 332 us (0.982)
  blocking collectives: 70.5 us -> 44.1 us
  waiting for transfers between devices: 107 us -> 118 us
  starting transfers between devices: 7.79 us -> 16.2 us
    all_gather x1 -> x0, blocking collectives: 27.8 us -> none  [on_device(): gathered = lax.all_gather(extract(extended), 'db', axis=1, tiled=True)]
    all_to_all x0 -> x1, starting transfers between devices: none -> 8.36 us  [on_device(): jax.lax.all_to_all(jnp.stack(jax.lax.axis_size('db') * [original], axis=0...]
    all_to_all x0 -> x1, waiting for transfers between devices: none -> 7.34 us  [on_device(): jax.lax.all_to_all(jnp.stack(jax.lax.axis_size('db') * [original], axis=0...]
  transfers between devices with their start and end apart: 3 -> 4, of which waited for: 2 -> 4; matrix products, arithmetic and copies ran while one was open for 6% -> 6% of each run, Pallas kernels for 0% -> 0%
where the time goes in v1:
time: 332 us; the launch traced here: 331 us
  waiting for transfers between devices  118 us (36%)
  matrix products  52.4 us (16%)
  other arithmetic  52.2 us (16%)
  blocking collectives  44.1 us (13%)
  local copies, waits for them, and re-layouts  28.1 us (8%)
  between operations  19.5 us (6%)
  starting transfers between devices  16.2 us (5%)
    all_gather x1, waiting for transfers between devices, combined_all(): everything = jax.tree.map(lambda part: lax.all_gather(part, axis), value)  109 us
    all_gather x2, blocking collectives, combined_all(): everything = jax.tree.map(lambda part: lax.all_gather(part, axis), value)  44.1 us
    add x15, other arithmetic, combine(): numerator = first[2] * factor_one[None, :] + second[2] * factor_two[None, :]  34 us
    dot_general x4, matrix products, on_device(): lax.dot_general(gathered, window, (((0,), (0,)), ((), ())), preferred_ele...  31.6 us
    dot_general x4, matrix products, on_device(): lax.dot_general(window, raw.astype(jnp.bfloat16), (((1,), (1,)), ((), ())...  20.8 us
    slice x144, local copies, waits for them, and re-layouts, extract(): pixels[:, :, row_shift:row_shift + height:4, col_shift:col_shift + across:4]  18.2 us
    reduce_sum x1, other arithmetic, on_device(): totals = totals * rescale + jnp.sum(raw, axis=1)  11.5 us
    all_to_all x1, starting transfers between devices, on_device(): jax.lax.all_to_all(jnp.stack(jax.lax.axis_size('db') * [original], axis=0...  8.36 us
  transfers between devices with their start and end apart: 4, of which 4 were waited for; matrix products, arithmetic and copies ran while one was open for 6% of the time, Pallas kernels for 0%

profile of v1, /device:TPU:1, one launch (start us, length us, event | category | flops | bytes accessed | tf_op | source)
XLA Modules:
  0.0 330.7 jit_solution(5302857340418467439)
XLA Ops:
  6.5 0.7 convert_element_type.45
  7.2 7.4 %collective-permute-start = (bf16[1,3,8,128]{3,2,1,0:T(8,128)(2,1)S(1)}, bf16[1,3,8,128]{3,2,1,0:T(8,128)(2,1)S(1)}, u32[]{:S(2)}, u32[]{:S(2)}) collective-permute-start(bf16[1,3,8,128]{3,2,1,0:T(8,128)(2,1)S(1)} %convert_element_type.45), channel_id=1, source_target_pairs={{0,240},{16,0},{32,16},{48,32},{64,48},{80,64},{96,80},{112,96},{1... | collective-permute-start | bytes 18440 | tf_op jit(solution)/shard_map/ppermute | solution.py:11
  14.8 0.6 collective-permute-done
  15.4 0.1 slice.610
  15.6 0.1 slice.598
  15.7 0.1 slice.586
  15.8 0.1 slice.574
  16.0 0.1 slice.562
  16.1 0.1 slice.634
  16.2 0.1 slice.622
  22.2 0.1 slice.643
  22.7 0.1 slice.639
  23.1 0.1 slice.636
  23.2 0.1 slice.635
  23.6 0.1 slice.631
  23.7 0.1 slice.630
  24.1 0.1 slice.627
  35.6 0.2 copy.4668
  35.8 0.1 stack_reshape.2
  36.0 1.1 stack.583
  37.1 8.4 %all-to-all-start = ((bf16[16,432,64]{1,2,0:T(8,128)(2,1)}), bf16[16,432,64]{1,2,0:T(8,128)(2,1)S(1)}, u32[]{:S(2)}, u32[]{:S(2)}) async-start(bf16[16,432,64]{1,2,0:T(8,128)(2,1)} %stack.583), calls=%async_computation | async-start | bytes 2097152 | tf_op jit(solution)/shard_map/all_to_all | solution.py:56
  45.5 1.5 fusion.44
  49.6 0.7 broadcast_in_dim.14
  50.4 4.7 %multiply_reduce_fusion.2 = (f32[2048]{0:T(1024)S(1)}, f32[2048]{0:T(1024)S(1)}, f32[2048]{0:T(1024)S(1)}, f32[2048]{0:T(1024)S(1)}) fusion(bf16[432,16384]{1,0:T(8,128)(2,1)} %param.14, s32[]{:T(128)S(6)} %select_n.33, s32[]{:T(128)S(6)} %select_n.32, s32[]{:T(128)S(6)} %select_n.34, s32[]{:T(128)S(6)} %select_n.35), kind=kLoop, calls=%fused_computation.33 | loop fusion | flops 10608640 | bytes 7110672 | tf_op jit(solution)/shard_map/reduce_sum | solution.py:75
  55.1 7.3 %all-to-all-done = bf16[16,432,64]{1,2,0:T(8,128)(2,1)S(1)} async-done(((bf16[16,432,64]{1,2,0:T(8,128)(2,1)}), bf16[16,432,64]{1,2,0:T(8,128)(2,1)S(1)}, u32[]{:S(2)}, u32[]{:S(2)}) %all-to-all-start) | async-done | bytes 884768 | tf_op jit(solution)/shard_map/all_to_all | solution.py:56
  62.4 3.8 %fusion.24 = f32[1024,2048]{1,0:T(8,128)S(1)} fusion(bf16[432,1024]{0,1:T(8,128)(2,1)S(1)} %bitcast.380, bf16[432,16384]{1,0:T(8,128)(2,1)} %param.14, s32[]{:T(128)S(6)} %select_n.35), kind=kOutput, calls=%fused_computation.37 | convolution fusion | flops 1811939328 | bytes 11042820 | tf_op jit(solution)/shard_map/dot_general | solution.py:76
  66.2 8.5 %fusion.27 = f32[1024,2048]{1,0:T(8,128)} fusion(bf16[432,1024]{0,1:T(8,128)(2,1)S(1)} %bitcast.381, bf16[432,16384]{1,0:T(8,128)(2,1)} %param.14, s32[]{:T(128)S(6)} %select_n.34), kind=kOutput, calls=%fused_computation.40 | convolution fusion | flops 1811939328 | bytes 11042820 | tf_op jit(solution)/shard_map/dot_general | solution.py:76
  74.7 6.4 %fusion.9 = (f32[1024]{0:T(1024)S(1)}, f32[1024,2048]{1,0:T(8,128)}) fusion(f32[2048]{0:T(1024)S(1)} %get-tuple-element.217, f32[1024]{0:T(1024)S(1)} %get-tuple-element.266, f32[1024]{0:T(1024)S(1)} %get-tuple-element.265, bf16[432,1024]{0,1:T(8,128)(2,1)S(1)} %bitcast.382, bf16[432,16384]{1,0:T(8,128)(2,1)} %param.14, s32[]{:T(128)S(6)} %select_n.32), kind=kOutput, calls=%fused_computation.23 | convolution fusion | flops 1820326912 | bytes 11063300 | tf_op jit(solution)/shard_map/dot_general | solution.py:76
  81.1 12.9 %fusion.2 = (f32[1024]{0:T(1024)S(1)}, f32[1024]{0:T(1024)S(1)}, f32[1024]{0:T(1024)S(1)}, f32[1024]{0:T(1024)S(1)}, f32[1024,2048]{1,0:T(8,128)}) fusion(f32[1024,2048]{1,0:T(8,128)} %get-tuple-element.272, f32[1024]{0:T(1024)S(1)} %get-tuple-element.271, f32[2048]{0:T(1024)S(1)} %get-tuple-element.217, f32[1024]{0:T(1024)S(1)} %get-tuple-element.266, ...), kind=kOutput, calls=%fused_computation.16 | convolution fusion | flops 1847586816 | bytes 36270084 | tf_op jit(solution)/shard_map/dot_general | solution.py:76
  94.0 5.8 %fusion.15 = f32[432,1024]{1,0:T(8,128)S(1)} fusion(f32[1024,2048]{1,0:T(8,128)} %fusion.27, f32[1024]{0:T(1024)S(1)} %get-tuple-element.248, f32[2048]{0:T(1024)S(1)} %get-tuple-element.218, f32[1024]{0:T(1024)S(1)} %get-tuple-element.266, f32[1024]{0:T(1024)S(1)} %get-tuple-element.265, bf16[432,16384]{1,0:T(8,128)(2,1)} %param.14, s32[]{:T(128)S(6)} %select_n.34), kind=kOutput, calls=%fused_computation.28 | convolution fusion | flops 1822425088 | bytes 11948036 | tf_op jit(solution)/shard_map/dot_general | solution.py:84
  99.9 4.3 %fusion.13 = f32[432,1024]{1,0:T(8,128)S(1)} fusion(f32[1024,2048]{1,0:T(8,128)S(1)} %fusion.24, f32[1024]{0:T(1024)S(1)} %get-tuple-element.250, f32[2048]{0:T(1024)S(1)} %get-tuple-element.219, f32[1024]{0:T(1024)S(1)} %get-tuple-element.266, f32[1024]{0:T(1024)S(1)} %get-tuple-element.265, bf16[432,16384]{1,0:T(8,128)(2,1)} %param.14, s32[]{:T(128)S(6)} %select_n.35), kind=kOutput, calls=%fused_computation.27 | convolution fusion | flops 1822425088 | bytes 11948036 | tf_op jit(solution)/shard_map/dot_general | solution.py:84
  104.3 4.3 %fusion.17 = f32[432,1024]{1,0:T(8,128)S(1)} fusion(f32[1024,2048]{1,0:T(8,128)S(1)} %bitcast.378, f32[1024]{0:T(1024)S(1)} %get-tuple-element.246, f32[2048]{0:T(1024)S(1)} %get-tuple-element.216, f32[1024]{0:T(1024)S(1)} %get-tuple-element.266, f32[1024]{0:T(1024)S(1)} %get-tuple-element.265, bf16[432,16384]{1,0:T(8,128)(2,1)} %param.14, s32[]{:T(128)S(6)} %select_n.33), kind=kOutput, calls=%fused_computation.29 | convolution fusion | flops 1822425088 | bytes 11948036 | tf_op jit(solution)/shard_map/dot_general | solution.py:84
  108.6 6.3 %multiply_add_fusion.1 = f32[432,1024]{1,0:T(8,128)} fusion(f32[432,1024]{1,0:T(8,128)S(1)} %fusion.13, f32[432,1024]{1,0:T(8,128)S(1)} %fusion.15, f32[432,1024]{1,0:T(8,128)S(1)} %fusion.17, f32[1024,2048]{1,0:T(8,128)S(1)} %bitcast.400, f32[1024]{0:T(1024)S(1)} %get-tuple-element.271, f32[2048]{0:T(1024)S(1)} %get-tuple-element.217, ...), kind=kOutput, calls=%fused_computation.35 | convolution fusion | flops 1825521664 | bytes 17272836 | tf_op jit(solution)/shard_map/dot_general | solution.py:84
  115.0 11.5 %fusion.4 = (f32[1024]{0:T(1024)S(1)}, f32[1024]{0:T(1024)S(1)}, f32[1024]{0:T(1024)S(1)}) fusion(f32[1024,2048]{1,0:T(8,128)} %get-tuple-element.273, f32[1024]{0:T(1024)S(1)} %get-tuple-element.246, f32[2048]{0:T(1024)S(1)} %get-tuple-element.216, f32[1024]{0:T(1024)S(1)} %get-tuple-element.266, f32[1024]{0:T(1024)S(1)} %get-tuple-element.265, ...), kind=kLoop, calls=%fused_computation.18 | loop fusion | flops 31454208 | bytes 25223168 | tf_op jit(solution)/shard_map/reduce_sum | solution.py:83
  126.5 21.0 %all-gather.2 = f32[16,1,1024]{2,1,0:T(1,128)S(1)} all-gather(f32[1,1,1024]{2,1,0:T(1,128)S(1)} %get-tuple-element.262), channel_id=1, replica_groups=mesh['query'=16,'db'=16] {'db'}, dimensions={0}, use_global_device_ids=true | all-gather | bytes 69632 | tf_op jit(solution)/shard_map/all_gather | solution.py:15
  147.5 23.1 %all-gather.1 = f32[16,1,1024]{2,1,0:T(1,128)S(1)} all-gather(f32[1,1,1024]{2,1,0:T(1,128)S(1)} %get-tuple-element.263), channel_id=1, replica_groups=mesh['query'=16,'db'=16] {'db'}, dimensions={0}, use_global_device_ids=true | all-gather | bytes 69632 | tf_op jit(solution)/shard_map/all_gather | solution.py:15
  170.6 109.4 %all-gather.5.cloned.1.call-done = f32[6912,1024]{1,0:T(8,128)} async-done(((f32[432,1024]{1,0:T(8,128)}), f32[6912,1024]{1,0:T(8,128)}) %all-gather.5.cloned.1.call-update) | async-done | bytes 28311568 | tf_op jit(solution)/shard_map/all_gather | solution.py:15
  280.0 1.6 slice.722
  281.6 34.9 %while.22 = (s32[]{:T(128)}, f32[1024]{0:T(1024)S(1)}, f32[1024]{0:T(1024)S(1)}, f32[432,1024]{1,0:T(8,128)S(1)}, f32[16,1024]{1,0:T(8,128)S(1)}, /*index=5*/f32...) while((s32[]{:T(128)}, f32[1024]{0:T(1024)S(1)}, f32[1024]{0:T(1024)S(1)}, ...), condition=%wide.region_13.0_spmd, body=%wide.region_12.0_spmd.sunk | while | flops 1333253 | bytes 5365903 | solution.py:21
  281.7 2.3 fusion.50
  284.0 2.3 fusion.50
  286.3 2.3 fusion.50
  288.7 2.3 fusion.50
  291.0 2.3 fusion.50
  293.3 2.3 fusion.50
  295.7 2.3 fusion.50
  298.0 2.3 fusion.50
  300.3 2.3 fusion.50
  302.7 2.3 fusion.50
  305.0 2.3 fusion.50
  307.3 2.3 fusion.50
  309.6 2.3 fusion.50
  312.0 2.3 fusion.50
  314.3 2.3 fusion.50
  316.8 0.3 reshape.306
  317.1 0.4 pad_add_fusion
  317.5 0.5 copy.4670
  318.0 0.3 reshape.307
  318.3 0.3 scatter-add.4
  318.5 0.4 collective-permute-start.1
  318.9 0.6 dynamic_slice.61
  320.9 0.6 dynamic_slice.60
  322.9 0.4 collective-permute-done.1
  323.3 0.6 multiply_add_fusion.2
  (344 shorter events, 19.2 us)
Async XLA Ops:
  7.2 8.2 %collective-permute-start = (bf16[1,3,8,128]{3,2,1,0:T(8,128)(2,1)S(1)}, bf16[1,3,8,128]{3,2,1,0:T(8,128)(2,1)S(1)}, u32[]{:S(2)}, u32[]{:S(2)}) collective-permute-start(bf16[1,3,8,128]{3,2,1,0:T(8,128)(2,1)S(1)} %convert_element_type.45), channel_id=1, source_target_pairs={{0,240},{16,0},{32,16},{48,32},{64,48},{80,64},{96,80},{112,96},{1... | collective-permute-start | bytes 18440 | tf_op jit(solution)/shard_map/ppermute | solution.py:11
  37.1 25.3 %all-to-all-start = ((bf16[16,432,64]{1,2,0:T(8,128)(2,1)}), bf16[16,432,64]{1,2,0:T(8,128)(2,1)S(1)}, u32[]{:S(2)}, u32[]{:S(2)}) async-start(bf16[16,432,64]{1,2,0:T(8,128)(2,1)} %stack.583), calls=%async_computation | async-start | bytes 2097152 | tf_op jit(solution)/shard_map/all_to_all | solution.py:56
  45.5 234.5 %all-gather.5.cloned.1.call-start = ((), (), s32[]{:S(2)}) async-start(), calls=%async_computation.1 | async-start | bytes 30081024 | tf_op jit(solution)/shard_map/all_gather | solution.py:15
  66.2 33.7 %copy-start = (f32[1024,2048]{1,0:T(8,128)}, f32[1024,2048]{1,0:T(8,128)S(1)}, u32[]{:S(2)}) copy-start(f32[1024,2048]{1,0:T(8,128)S(1)} %fusion.24) | copy-start | bytes 25165828
  94.0 10.2 %slice-start = ((s8[8388608]{0:T(1024)(128)(4,1)}), s8[4194304]{0:T(1024)(128)(4,1)S(1)}, s32[]{:S(2)}) async-start(s8[8388608]{0:T(1024)(128)(4,1)} %bitcast.377), calls=%async_computation.2 | async-start | bytes 8388608
  99.9 4.4 %slice-start.1 = ((s8[8388608]{0:T(1024)(128)(4,1)}), s8[4194304]{0:T(1024)(128)(4,1)S(1)}, s32[]{:S(2)}) async-start(s8[8388608]{0:T(1024)(128)(4,1)} %bitcast.377), calls=%async_computation.3 | async-start | bytes 8388608
  99.9 8.7 %slice-start.2 = ((s8[8388608]{0:T(1024)(128)(4,1)}), s8[4194304]{0:T(1024)(128)(4,1)S(1)}, s32[]{:S(2)}) async-start(s8[8388608]{0:T(1024)(128)(4,1)} %bitcast.399), calls=%async_computation.4 | async-start | bytes 8388608
  104.3 4.3 %slice-start.3 = ((s8[8388608]{0:T(1024)(128)(4,1)}), s8[4194304]{0:T(1024)(128)(4,1)S(1)}, s32[]{:S(2)}) async-start(s8[8388608]{0:T(1024)(128)(4,1)} %bitcast.399), calls=%async_computation.5 | async-start | bytes 8388608
  281.6 37.3 %copy-start.2 = (f32[16]{0:T(128)S(1)}, f32[16]{0:T(128)}, u32[]{:S(2)}) copy-start(f32[16]{0:T(128)} %param.16) | copy-start | bytes 196
  281.6 39.2 %copy-start.3 = (f32[16]{0:T(128)S(1)}, f32[16]{0:T(128)}, u32[]{:S(2)}) copy-start(f32[16]{0:T(128)} %param.17) | copy-start | bytes 196
  281.6 41.7 %copy-start.1 = (f32[1,3,8,128]{3,2,1,0:T(8,128)S(1)}, f32[1,3,8,128]{3,2,1,0:T(8,128)}, u32[]{:S(2)}) copy-start(f32[1,3,8,128]{3,2,1,0:T(8,128)} %param.13) | copy-start | bytes 36868
  318.5 4.7 %collective-permute-start.1 = (f32[1,3,8,128]{3,2,1,0:T(8,128)S(1)}, f32[1,3,8,128]{3,2,1,0:T(8,128)S(1)}, u32[]{:S(2)}, u32[]{:S(2)}) collective-permute-start(f32[1,3,8,128]{3,2,1,0:T(8,128)S(1)} %slice.736), channel_id=1, source_target_pairs={{0,16},{16,32},{32,48},{48,64},{64,80},{80,96},{96,112},{112,128},... | collective-permute-start | bytes 36872 | tf_op jit(solution)/shard_map/ppermute | solution.py:11
Sparse Core Ops, SparseCore 0:
  115.1 164.8 all-gather.4
